TPU v7x, 768 devices: a whole 4x8x12 slice. The times are simulated.
768 devices in a mesh: blk: 24 (over z, y_hi), section: 32 (over y_lo, x, core).
Axes of the slice: x: 4, y: 8 (y_hi: 2, y_lo: 4; y = y_hi * 4 + y_lo), z: 12, core: 2. Of those that a mesh axis runs over, the one named last changes fastest.
Arguments:
- text_emb: bfloat16 [32, 6144, 1024], P(None, ('blk', 'section')), may hold values from -6 to 6
- covariate: bfloat16 [32, 1536, 1024], P('section', 'blk'), may hold values from -6 to 6
- labels: int32 [32, 6144], P('section', 'blk'), may hold values from 0 to 1535, as said below
- logit_scale: float32 [1], replicated, may hold values from 0.02 to 0.08
- logit_bias: float32 [1], replicated, may hold values from -3 to -1
Outputs:
- text_grad: float32 [32, 6144, 1024], P('section', 'blk')
- cov_grad: float32 [32, 1536, 1024], P('section', 'blk')
Inputs may be any that keep to these rules, and one draw needn't show every extreme that they name: `labels`: every covariate row of a group is the positive of exactly 4 text rows of that group.
All inputs are finite; a program needn't handle non-finite values.
Results may differ from a plain program's by a relative error of at most 0.0025.
Values may be sent and summed in bfloat16 or wider, within the bound.
A program may use at most 32 MiB of HBM per device.

v0:
```python
import jax
import jax.numpy as jnp
from jax import lax
from jax.sharding import PartitionSpec as P


def shifted_2(value, axis, steps):
    count = lax.axis_size(axis)
    pairs = [(source, (source + steps) % count) for source in range(count)]
    return lax.ppermute(value, axis, pairs)


def local(text_emb, covariate, labels, logit_scale, logit_bias):
    panel = lax.all_to_all(text_emb, "section", split_axis=0, concat_axis=1, tiled=True)[0]
    cov_own = covariate[0]
    row_labels = labels[0]
    cycle_len = lax.axis_size("blk")
    cycle_pos = lax.axis_index("blk")
    piece_rows = cov_own.shape[0]
    factor = logit_scale[0]
    offset = logit_bias[0]
    local_ids = jnp.arange(piece_rows, dtype=jnp.int32)

    def cycle_step(carry, visits):
        cov_piece, running, text_acc = carry
        source = (cycle_pos - visits) % cycle_len
        logits = (
            factor
            * lax.dot_general(
                cov_piece, panel, (((1,), (1,)), ((), ())), preferred_element_type=jnp.float32
            )
            + offset
        )
        row_ids = source * piece_rows + local_ids
        positive = (row_labels[None, :] == row_ids[:, None]).astype(jnp.float32)
        weights_bf = (factor * (jax.nn.sigmoid(logits) - positive)).astype(jnp.bfloat16)
        cov_term = jnp.dot(weights_bf, panel, preferred_element_type=jnp.float32)
        text_acc = text_acc + lax.dot_general(
            weights_bf, cov_piece, (((0,), (0,)), ((), ())), preferred_element_type=jnp.float32
        )
        shifted = shifted_2(cov_piece, "blk", 1)
        running = shifted_2(running + cov_term, "blk", 1)
        saved = jnp.zeros((), jnp.float32)
        return ((shifted, running, text_acc), saved)

    start_sum = jnp.zeros(cov_own.shape, jnp.float32)
    start_text = jnp.zeros(panel.shape, jnp.float32)
    (final_piece, running, text_grad), saved = lax.scan(
        cycle_step, (cov_own, start_sum, start_text), jnp.arange(cycle_len, dtype=jnp.int32)
    )
    return (text_grad[None], running[None])


def solution(mesh):
    return jax.shard_map(
        local,
        mesh=mesh,
        in_specs=(
            P(None, ("blk", "section"), None),
            P("section", "blk", None),
            P("section", "blk"),
            P(),
            P(),
        ),
        out_specs=(P("section", "blk", None), P("section", "blk", None)),
        check_vma=False,
    )
```

profile of v0, /device:TPU:104, one launch (start us, length us, event | category | flops | bytes accessed | tf_op | source)
XLA Modules:
  0.0 647.5 jit_solution(605326373021406898)
XLA Ops:
  0.6 6.2 all-to-all-start
  6.8 15.4 %all-to-all-done = bf16[32,8,1024]{2,1,0:T(8,128)(2,1)S(1)} async-done(((bf16[32,8,1024]{2,1,0:T(8,128)(2,1)}), bf16[32,8,1024]{2,1,0:T(8,128)(2,1)S(1)}, u32[]{:S(2)}, u32[]{:S(2)}) %all-to-all-start) | async-done | bytes 524320 | tf_op jit(solution)/shard_map/all_to_all | solution.py:14
  23.1 623.4 %while.17 = (s32[]{:T(128)}, bf16[64,1024]{1,0:T(8,128)(2,1)S(1)}, f32[64,1024]{1,0:T(8,128)S(1)}, f32[256,1024]{1,0:T(8,128)S(1)}, f32[]{:T(128)}, /*index=5*/b...) while((s32[]{:T(128)}, bf16[64,1024]{1,0:T(8,128)(2,1)S(1)}, ...), condition=%wide.region_1.2_spmd.clone, body=%wide.region_0.1_spmd.clone.sunk | while | flops 101417032 | bytes 5867337 | solution.py:48
  23.1 6.5 %collective-permute-start = (bf16[64,1024]{1,0:T(8,128)(2,1)S(1)}, bf16[64,1024]{1,0:T(8,128)(2,1)S(1)}, u32[]{:S(2)}, u32[]{:S(2)}) collective-permute-start(bf16[64,1024]{1,0:T(8,128)(2,1)S(1)} %copy.12), channel_id=1, source_target_pairs={{0,32},{32,64},{64,96},{96,128},{128,160},{160,192},{192,224},{224... | collective-permute-start | bytes 393224 | tf_op jit(solution)/shard_map/while/body/eval_jaxpr/ppermute | solution.py:10
  38.1 14.3 %collective-permute-done.1 = f32[64,1024]{1,0:T(8,128)S(1)} collective-permute-done((f32[64,1024]{1,0:T(8,128)S(1)}, f32[64,1024]{1,0:T(8,128)S(1)}, u32[]{:S(2)}, u32[]{:S(2)}) %collective-permute-start.1) | collective-permute-done | bytes 262176 | tf_op jit(solution)/shard_map/while/body/eval_jaxpr/ppermute | solution.py:10
  52.4 5.9 collective-permute-start
  67.4 11.6 %collective-permute-done.1 = f32[64,1024]{1,0:T(8,128)S(1)} collective-permute-done((f32[64,1024]{1,0:T(8,128)S(1)}, f32[64,1024]{1,0:T(8,128)S(1)}, u32[]{:S(2)}, u32[]{:S(2)}) %collective-permute-start.1) | collective-permute-done | bytes 262176 | tf_op jit(solution)/shard_map/while/body/eval_jaxpr/ppermute | solution.py:10
  79.0 7.4 %collective-permute-start = (bf16[64,1024]{1,0:T(8,128)(2,1)S(1)}, bf16[64,1024]{1,0:T(8,128)(2,1)S(1)}, u32[]{:S(2)}, u32[]{:S(2)}) collective-permute-start(bf16[64,1024]{1,0:T(8,128)(2,1)S(1)} %copy.12), channel_id=1, source_target_pairs={{0,32},{32,64},{64,96},{96,128},{128,160},{160,192},{192,224},{224... | collective-permute-start | bytes 393224 | tf_op jit(solution)/shard_map/while/body/eval_jaxpr/ppermute | solution.py:10
  93.9 11.8 %collective-permute-done.1 = f32[64,1024]{1,0:T(8,128)S(1)} collective-permute-done((f32[64,1024]{1,0:T(8,128)S(1)}, f32[64,1024]{1,0:T(8,128)S(1)}, u32[]{:S(2)}, u32[]{:S(2)}) %collective-permute-start.1) | collective-permute-done | bytes 262176 | tf_op jit(solution)/shard_map/while/body/eval_jaxpr/ppermute | solution.py:10
  118.1 11.7 %collective-permute-done.1 = f32[64,1024]{1,0:T(8,128)S(1)} collective-permute-done((f32[64,1024]{1,0:T(8,128)S(1)}, f32[64,1024]{1,0:T(8,128)S(1)}, u32[]{:S(2)}, u32[]{:S(2)}) %collective-permute-start.1) | collective-permute-done | bytes 262176 | tf_op jit(solution)/shard_map/while/body/eval_jaxpr/ppermute | solution.py:10
  129.8 7.3 %collective-permute-start = (bf16[64,1024]{1,0:T(8,128)(2,1)S(1)}, bf16[64,1024]{1,0:T(8,128)(2,1)S(1)}, u32[]{:S(2)}, u32[]{:S(2)}) collective-permute-start(bf16[64,1024]{1,0:T(8,128)(2,1)S(1)} %copy.12), channel_id=1, source_target_pairs={{0,32},{32,64},{64,96},{96,128},{128,160},{160,192},{192,224},{224... | collective-permute-start | bytes 393224 | tf_op jit(solution)/shard_map/while/body/eval_jaxpr/ppermute | solution.py:10
  140.1 8.4 %collective-permute-start.1 = (f32[64,1024]{1,0:T(8,128)S(1)}, f32[64,1024]{1,0:T(8,128)S(1)}, u32[]{:S(2)}, u32[]{:S(2)}) collective-permute-start(f32[64,1024]{1,0:T(8,128)S(1)} %convolution_add_fusion.4), channel_id=1, source_target_pairs={{0,32},{32,64},{64,96},{96,128},{128,160},{160,192},{192,224},{224... | collective-permute-start | bytes 786440 | tf_op jit(solution)/shard_map/while/body/eval_jaxpr/ppermute | solution.py:10
  154.2 9.2 %collective-permute-start = (bf16[64,1024]{1,0:T(8,128)(2,1)S(1)}, bf16[64,1024]{1,0:T(8,128)(2,1)S(1)}, u32[]{:S(2)}, u32[]{:S(2)}) collective-permute-start(bf16[64,1024]{1,0:T(8,128)(2,1)S(1)} %copy.12), channel_id=1, source_target_pairs={{0,32},{32,64},{64,96},{96,128},{128,160},{160,192},{192,224},{224... | collective-permute-start | bytes 393224 | tf_op jit(solution)/shard_map/while/body/eval_jaxpr/ppermute | solution.py:10
  166.5 6.5 collective-permute-start.1
  173.4 10.1 %collective-permute-done.1 = f32[64,1024]{1,0:T(8,128)S(1)} collective-permute-done((f32[64,1024]{1,0:T(8,128)S(1)}, f32[64,1024]{1,0:T(8,128)S(1)}, u32[]{:S(2)}, u32[]{:S(2)}) %collective-permute-start.1) | collective-permute-done | bytes 262176 | tf_op jit(solution)/shard_map/while/body/eval_jaxpr/ppermute | solution.py:10
  190.8 6.4 collective-permute-start.1
  197.7 11.5 %collective-permute-done.1 = f32[64,1024]{1,0:T(8,128)S(1)} collective-permute-done((f32[64,1024]{1,0:T(8,128)S(1)}, f32[64,1024]{1,0:T(8,128)S(1)}, u32[]{:S(2)}, u32[]{:S(2)}) %collective-permute-start.1) | collective-permute-done | bytes 262176 | tf_op jit(solution)/shard_map/while/body/eval_jaxpr/ppermute | solution.py:10
  220.0 6.4 collective-permute-done
  226.4 6.9 %collective-permute-done.1 = f32[64,1024]{1,0:T(8,128)S(1)} collective-permute-done((f32[64,1024]{1,0:T(8,128)S(1)}, f32[64,1024]{1,0:T(8,128)S(1)}, u32[]{:S(2)}, u32[]{:S(2)}) %collective-permute-start.1) | collective-permute-done | bytes 262176 | tf_op jit(solution)/shard_map/while/body/eval_jaxpr/ppermute | solution.py:10
  246.4 9.9 %collective-permute-done.1 = f32[64,1024]{1,0:T(8,128)S(1)} collective-permute-done((f32[64,1024]{1,0:T(8,128)S(1)}, f32[64,1024]{1,0:T(8,128)S(1)}, u32[]{:S(2)}, u32[]{:S(2)}) %collective-permute-start.1) | collective-permute-done | bytes 262176 | tf_op jit(solution)/shard_map/while/body/eval_jaxpr/ppermute | solution.py:10
  256.4 6.8 %collective-permute-start = (bf16[64,1024]{1,0:T(8,128)(2,1)S(1)}, bf16[64,1024]{1,0:T(8,128)(2,1)S(1)}, u32[]{:S(2)}, u32[]{:S(2)}) collective-permute-start(bf16[64,1024]{1,0:T(8,128)(2,1)S(1)} %copy.12), channel_id=1, source_target_pairs={{0,32},{32,64},{64,96},{96,128},{128,160},{160,192},{192,224},{224... | collective-permute-start | bytes 393224 | tf_op jit(solution)/shard_map/while/body/eval_jaxpr/ppermute | solution.py:10
  266.1 8.3 %collective-permute-start.1 = (f32[64,1024]{1,0:T(8,128)S(1)}, f32[64,1024]{1,0:T(8,128)S(1)}, u32[]{:S(2)}, u32[]{:S(2)}) collective-permute-start(f32[64,1024]{1,0:T(8,128)S(1)} %convolution_add_fusion.4), channel_id=1, source_target_pairs={{0,32},{32,64},{64,96},{96,128},{128,160},{160,192},{192,224},{224... | collective-permute-start | bytes 786440 | tf_op jit(solution)/shard_map/while/body/eval_jaxpr/ppermute | solution.py:10
  274.8 8.2 %collective-permute-done.1 = f32[64,1024]{1,0:T(8,128)S(1)} collective-permute-done((f32[64,1024]{1,0:T(8,128)S(1)}, f32[64,1024]{1,0:T(8,128)S(1)}, u32[]{:S(2)}, u32[]{:S(2)}) %collective-permute-start.1) | collective-permute-done | bytes 262176 | tf_op jit(solution)/shard_map/while/body/eval_jaxpr/ppermute | solution.py:10
  283.1 9.3 %collective-permute-start = (bf16[64,1024]{1,0:T(8,128)(2,1)S(1)}, bf16[64,1024]{1,0:T(8,128)(2,1)S(1)}, u32[]{:S(2)}, u32[]{:S(2)}) collective-permute-start(bf16[64,1024]{1,0:T(8,128)(2,1)S(1)} %copy.12), channel_id=1, source_target_pairs={{0,32},{32,64},{64,96},{96,128},{128,160},{160,192},{192,224},{224... | collective-permute-start | bytes 393224 | tf_op jit(solution)/shard_map/while/body/eval_jaxpr/ppermute | solution.py:10
  301.2 12.9 %collective-permute-done.1 = f32[64,1024]{1,0:T(8,128)S(1)} collective-permute-done((f32[64,1024]{1,0:T(8,128)S(1)}, f32[64,1024]{1,0:T(8,128)S(1)}, u32[]{:S(2)}, u32[]{:S(2)}) %collective-permute-start.1) | collective-permute-done | bytes 262176 | tf_op jit(solution)/shard_map/while/body/eval_jaxpr/ppermute | solution.py:10
  321.6 8.3 %collective-permute-start.1 = (f32[64,1024]{1,0:T(8,128)S(1)}, f32[64,1024]{1,0:T(8,128)S(1)}, u32[]{:S(2)}, u32[]{:S(2)}) collective-permute-start(f32[64,1024]{1,0:T(8,128)S(1)} %convolution_add_fusion.4), channel_id=1, source_target_pairs={{0,32},{32,64},{64,96},{96,128},{128,160},{160,192},{192,224},{224... | collective-permute-start | bytes 786440 | tf_op jit(solution)/shard_map/while/body/eval_jaxpr/ppermute | solution.py:10
  330.4 11.6 %collective-permute-done.1 = f32[64,1024]{1,0:T(8,128)S(1)} collective-permute-done((f32[64,1024]{1,0:T(8,128)S(1)}, f32[64,1024]{1,0:T(8,128)S(1)}, u32[]{:S(2)}, u32[]{:S(2)}) %collective-permute-start.1) | collective-permute-done | bytes 262176 | tf_op jit(solution)/shard_map/while/body/eval_jaxpr/ppermute | solution.py:10
  342.0 8.0 %collective-permute-start = (bf16[64,1024]{1,0:T(8,128)(2,1)S(1)}, bf16[64,1024]{1,0:T(8,128)(2,1)S(1)}, u32[]{:S(2)}, u32[]{:S(2)}) collective-permute-start(bf16[64,1024]{1,0:T(8,128)(2,1)S(1)} %copy.12), channel_id=1, source_target_pairs={{0,32},{32,64},{64,96},{96,128},{128,160},{160,192},{192,224},{224... | collective-permute-start | bytes 393224 | tf_op jit(solution)/shard_map/while/body/eval_jaxpr/ppermute | solution.py:10
  355.8 15.1 %collective-permute-done.1 = f32[64,1024]{1,0:T(8,128)S(1)} collective-permute-done((f32[64,1024]{1,0:T(8,128)S(1)}, f32[64,1024]{1,0:T(8,128)S(1)}, u32[]{:S(2)}, u32[]{:S(2)}) %collective-permute-start.1) | collective-permute-done | bytes 262176 | tf_op jit(solution)/shard_map/while/body/eval_jaxpr/ppermute | solution.py:10
  380.0 11.0 %collective-permute-done = bf16[64,1024]{1,0:T(8,128)(2,1)S(1)} collective-permute-done((bf16[64,1024]{1,0:T(8,128)(2,1)S(1)}, bf16[64,1024]{1,0:T(8,128)(2,1)S(1)}, u32[]{:S(2)}, u32[]{:S(2)}) %collective-permute-start) | collective-permute-done | bytes 131104 | tf_op jit(solution)/shard_map/while/body/eval_jaxpr/ppermute | solution.py:10
  409.4 8.2 %collective-permute-done.1 = f32[64,1024]{1,0:T(8,128)S(1)} collective-permute-done((f32[64,1024]{1,0:T(8,128)S(1)}, f32[64,1024]{1,0:T(8,128)S(1)}, u32[]{:S(2)}, u32[]{:S(2)}) %collective-permute-start.1) | collective-permute-done | bytes 262176 | tf_op jit(solution)/shard_map/while/body/eval_jaxpr/ppermute | solution.py:10
  422.6 6.0 collective-permute-start.1
  431.0 9.6 %collective-permute-done.1 = f32[64,1024]{1,0:T(8,128)S(1)} collective-permute-done((f32[64,1024]{1,0:T(8,128)S(1)}, f32[64,1024]{1,0:T(8,128)S(1)}, u32[]{:S(2)}, u32[]{:S(2)}) %collective-permute-start.1) | collective-permute-done | bytes 262176 | tf_op jit(solution)/shard_map/while/body/eval_jaxpr/ppermute | solution.py:10
  454.9 10.5 %collective-permute-done.1 = f32[64,1024]{1,0:T(8,128)S(1)} collective-permute-done((f32[64,1024]{1,0:T(8,128)S(1)}, f32[64,1024]{1,0:T(8,128)S(1)}, u32[]{:S(2)}, u32[]{:S(2)}) %collective-permute-start.1) | collective-permute-done | bytes 262176 | tf_op jit(solution)/shard_map/while/body/eval_jaxpr/ppermute | solution.py:10
  474.0 7.1 %collective-permute-start.1 = (f32[64,1024]{1,0:T(8,128)S(1)}, f32[64,1024]{1,0:T(8,128)S(1)}, u32[]{:S(2)}, u32[]{:S(2)}) collective-permute-start(f32[64,1024]{1,0:T(8,128)S(1)} %convolution_add_fusion.4), channel_id=1, source_target_pairs={{0,32},{32,64},{64,96},{96,128},{128,160},{160,192},{192,224},{224... | collective-permute-start | bytes 786440 | tf_op jit(solution)/shard_map/while/body/eval_jaxpr/ppermute | solution.py:10
  481.6 13.6 %collective-permute-done.1 = f32[64,1024]{1,0:T(8,128)S(1)} collective-permute-done((f32[64,1024]{1,0:T(8,128)S(1)}, f32[64,1024]{1,0:T(8,128)S(1)}, u32[]{:S(2)}, u32[]{:S(2)}) %collective-permute-start.1) | collective-permute-done | bytes 262176 | tf_op jit(solution)/shard_map/while/body/eval_jaxpr/ppermute | solution.py:10
  504.3 11.1 %collective-permute-done = bf16[64,1024]{1,0:T(8,128)(2,1)S(1)} collective-permute-done((bf16[64,1024]{1,0:T(8,128)(2,1)S(1)}, bf16[64,1024]{1,0:T(8,128)(2,1)S(1)}, u32[]{:S(2)}, u32[]{:S(2)}) %collective-permute-start) | collective-permute-done | bytes 131104 | tf_op jit(solution)/shard_map/while/body/eval_jaxpr/ppermute | solution.py:10
  515.4 6.1 collective-permute-done.1
  528.8 8.9 %collective-permute-done = bf16[64,1024]{1,0:T(8,128)(2,1)S(1)} collective-permute-done((bf16[64,1024]{1,0:T(8,128)(2,1)S(1)}, bf16[64,1024]{1,0:T(8,128)(2,1)S(1)}, u32[]{:S(2)}, u32[]{:S(2)}) %collective-permute-start) | collective-permute-done | bytes 131104 | tf_op jit(solution)/shard_map/while/body/eval_jaxpr/ppermute | solution.py:10
  537.7 7.5 %collective-permute-done.1 = f32[64,1024]{1,0:T(8,128)S(1)} collective-permute-done((f32[64,1024]{1,0:T(8,128)S(1)}, f32[64,1024]{1,0:T(8,128)S(1)}, u32[]{:S(2)}, u32[]{:S(2)}) %collective-permute-start.1) | collective-permute-done | bytes 262176 | tf_op jit(solution)/shard_map/while/body/eval_jaxpr/ppermute | solution.py:10
  552.5 10.5 %collective-permute-done = bf16[64,1024]{1,0:T(8,128)(2,1)S(1)} collective-permute-done((bf16[64,1024]{1,0:T(8,128)(2,1)S(1)}, bf16[64,1024]{1,0:T(8,128)(2,1)S(1)}, u32[]{:S(2)}, u32[]{:S(2)}) %collective-permute-start) | collective-permute-done | bytes 131104 | tf_op jit(solution)/shard_map/while/body/eval_jaxpr/ppermute | solution.py:10
  562.9 6.9 %collective-permute-done.1 = f32[64,1024]{1,0:T(8,128)S(1)} collective-permute-done((f32[64,1024]{1,0:T(8,128)S(1)}, f32[64,1024]{1,0:T(8,128)S(1)}, u32[]{:S(2)}, u32[]{:S(2)}) %collective-permute-start.1) | collective-permute-done | bytes 262176 | tf_op jit(solution)/shard_map/while/body/eval_jaxpr/ppermute | solution.py:10
  581.5 10.1 %collective-permute-done.1 = f32[64,1024]{1,0:T(8,128)S(1)} collective-permute-done((f32[64,1024]{1,0:T(8,128)S(1)}, f32[64,1024]{1,0:T(8,128)S(1)}, u32[]{:S(2)}, u32[]{:S(2)}) %collective-permute-start.1) | collective-permute-done | bytes 262176 | tf_op jit(solution)/shard_map/while/body/eval_jaxpr/ppermute | solution.py:10
  591.6 8.8 %collective-permute-start = (bf16[64,1024]{1,0:T(8,128)(2,1)S(1)}, bf16[64,1024]{1,0:T(8,128)(2,1)S(1)}, u32[]{:S(2)}, u32[]{:S(2)}) collective-permute-start(bf16[64,1024]{1,0:T(8,128)(2,1)S(1)} %copy.12), channel_id=1, source_target_pairs={{0,32},{32,64},{64,96},{96,128},{128,160},{160,192},{192,224},{224... | collective-permute-start | bytes 393224 | tf_op jit(solution)/shard_map/while/body/eval_jaxpr/ppermute | solution.py:10
  603.4 8.4 %collective-permute-start.1 = (f32[64,1024]{1,0:T(8,128)S(1)}, f32[64,1024]{1,0:T(8,128)S(1)}, u32[]{:S(2)}, u32[]{:S(2)}) collective-permute-start(f32[64,1024]{1,0:T(8,128)S(1)} %convolution_add_fusion.4), channel_id=1, source_target_pairs={{0,32},{32,64},{64,96},{96,128},{128,160},{160,192},{192,224},{224... | collective-permute-start | bytes 786440 | tf_op jit(solution)/shard_map/while/body/eval_jaxpr/ppermute | solution.py:10
  612.2 6.6 %collective-permute-done.1 = f32[64,1024]{1,0:T(8,128)S(1)} collective-permute-done((f32[64,1024]{1,0:T(8,128)S(1)}, f32[64,1024]{1,0:T(8,128)S(1)}, u32[]{:S(2)}, u32[]{:S(2)}) %collective-permute-start.1) | collective-permute-done | bytes 262176 | tf_op jit(solution)/shard_map/while/body/eval_jaxpr/ppermute | solution.py:10
  618.8 9.7 %collective-permute-start = (bf16[64,1024]{1,0:T(8,128)(2,1)S(1)}, bf16[64,1024]{1,0:T(8,128)(2,1)S(1)}, u32[]{:S(2)}, u32[]{:S(2)}) collective-permute-start(bf16[64,1024]{1,0:T(8,128)(2,1)S(1)} %copy.12), channel_id=1, source_target_pairs={{0,32},{32,64},{64,96},{96,128},{128,160},{160,192},{192,224},{224... | collective-permute-start | bytes 393224 | tf_op jit(solution)/shard_map/while/body/eval_jaxpr/ppermute | solution.py:10
  633.8 12.6 %collective-permute-done.1 = f32[64,1024]{1,0:T(8,128)S(1)} collective-permute-done((f32[64,1024]{1,0:T(8,128)S(1)}, f32[64,1024]{1,0:T(8,128)S(1)}, u32[]{:S(2)}, u32[]{:S(2)}) %collective-permute-start.1) | collective-permute-done | bytes 262176 | tf_op jit(solution)/shard_map/while/body/eval_jaxpr/ppermute | solution.py:10
  (205 shorter events, 196.5 us)
Async XLA Ops:
  0.6 21.5 %all-to-all-start = ((bf16[32,8,1024]{2,1,0:T(8,128)(2,1)}), bf16[32,8,1024]{2,1,0:T(8,128)(2,1)S(1)}, u32[]{:S(2)}, u32[]{:S(2)}) async-start(bf16[32,8,1024]{2,1,0:T(8,128)(2,1)} %param.7), calls=%async_computation | async-start | bytes 1048576 | tf_op jit(solution)/shard_map/all_to_all | solution.py:14
  23.1 15.0 %collective-permute-start = (bf16[64,1024]{1,0:T(8,128)(2,1)S(1)}, bf16[64,1024]{1,0:T(8,128)(2,1)S(1)}, u32[]{:S(2)}, u32[]{:S(2)}) collective-permute-start(bf16[64,1024]{1,0:T(8,128)(2,1)S(1)} %copy.12), channel_id=1, source_target_pairs={{0,32},{32,64},{64,96},{96,128},{128,160},{160,192},{192,224},{224... | collective-permute-start | bytes 393224 | tf_op jit(solution)/shard_map/while/body/eval_jaxpr/ppermute | solution.py:10
  32.6 19.8 %collective-permute-start.1 = (f32[64,1024]{1,0:T(8,128)S(1)}, f32[64,1024]{1,0:T(8,128)S(1)}, u32[]{:S(2)}, u32[]{:S(2)}) collective-permute-start(f32[64,1024]{1,0:T(8,128)S(1)} %convolution_add_fusion.4), channel_id=1, source_target_pairs={{0,32},{32,64},{64,96},{96,128},{128,160},{160,192},{192,224},{224... | collective-permute-start | bytes 786440 | tf_op jit(solution)/shard_map/while/body/eval_jaxpr/ppermute | solution.py:10
  52.4 15.0 %collective-permute-start = (bf16[64,1024]{1,0:T(8,128)(2,1)S(1)}, bf16[64,1024]{1,0:T(8,128)(2,1)S(1)}, u32[]{:S(2)}, u32[]{:S(2)}) collective-permute-start(bf16[64,1024]{1,0:T(8,128)(2,1)S(1)} %copy.12), channel_id=1, source_target_pairs={{0,32},{32,64},{64,96},{96,128},{128,160},{160,192},{192,224},{224... | collective-permute-start | bytes 393224 | tf_op jit(solution)/shard_map/while/body/eval_jaxpr/ppermute | solution.py:10
  61.4 17.6 %collective-permute-start.1 = (f32[64,1024]{1,0:T(8,128)S(1)}, f32[64,1024]{1,0:T(8,128)S(1)}, u32[]{:S(2)}, u32[]{:S(2)}) collective-permute-start(f32[64,1024]{1,0:T(8,128)S(1)} %convolution_add_fusion.4), channel_id=1, source_target_pairs={{0,32},{32,64},{64,96},{96,128},{128,160},{160,192},{192,224},{224... | collective-permute-start | bytes 786440 | tf_op jit(solution)/shard_map/while/body/eval_jaxpr/ppermute | solution.py:10
  79.0 14.9 %collective-permute-start = (bf16[64,1024]{1,0:T(8,128)(2,1)S(1)}, bf16[64,1024]{1,0:T(8,128)(2,1)S(1)}, u32[]{:S(2)}, u32[]{:S(2)}) collective-permute-start(bf16[64,1024]{1,0:T(8,128)(2,1)S(1)} %copy.12), channel_id=1, source_target_pairs={{0,32},{32,64},{64,96},{96,128},{128,160},{160,192},{192,224},{224... | collective-permute-start | bytes 393224 | tf_op jit(solution)/shard_map/while/body/eval_jaxpr/ppermute | solution.py:10
  89.4 16.4 %collective-permute-start.1 = (f32[64,1024]{1,0:T(8,128)S(1)}, f32[64,1024]{1,0:T(8,128)S(1)}, u32[]{:S(2)}, u32[]{:S(2)}) collective-permute-start(f32[64,1024]{1,0:T(8,128)S(1)} %convolution_add_fusion.4), channel_id=1, source_target_pairs={{0,32},{32,64},{64,96},{96,128},{128,160},{160,192},{192,224},{224... | collective-permute-start | bytes 786440 | tf_op jit(solution)/shard_map/while/body/eval_jaxpr/ppermute | solution.py:10
  105.8 12.3 %collective-permute-start = (bf16[64,1024]{1,0:T(8,128)(2,1)S(1)}, bf16[64,1024]{1,0:T(8,128)(2,1)S(1)}, u32[]{:S(2)}, u32[]{:S(2)}) collective-permute-start(bf16[64,1024]{1,0:T(8,128)(2,1)S(1)} %copy.12), channel_id=1, source_target_pairs={{0,32},{32,64},{64,96},{96,128},{128,160},{160,192},{192,224},{224... | collective-permute-start | bytes 393224 | tf_op jit(solution)/shard_map/while/body/eval_jaxpr/ppermute | solution.py:10
  113.3 16.5 %collective-permute-start.1 = (f32[64,1024]{1,0:T(8,128)S(1)}, f32[64,1024]{1,0:T(8,128)S(1)}, u32[]{:S(2)}, u32[]{:S(2)}) collective-permute-start(f32[64,1024]{1,0:T(8,128)S(1)} %convolution_add_fusion.4), channel_id=1, source_target_pairs={{0,32},{32,64},{64,96},{96,128},{128,160},{160,192},{192,224},{224... | collective-permute-start | bytes 786440 | tf_op jit(solution)/shard_map/while/body/eval_jaxpr/ppermute | solution.py:10
  129.8 19.1 %collective-permute-start = (bf16[64,1024]{1,0:T(8,128)(2,1)S(1)}, bf16[64,1024]{1,0:T(8,128)(2,1)S(1)}, u32[]{:S(2)}, u32[]{:S(2)}) collective-permute-start(bf16[64,1024]{1,0:T(8,128)(2,1)S(1)} %copy.12), channel_id=1, source_target_pairs={{0,32},{32,64},{64,96},{96,128},{128,160},{160,192},{192,224},{224... | collective-permute-start | bytes 393224 | tf_op jit(solution)/shard_map/while/body/eval_jaxpr/ppermute | solution.py:10
  140.1 14.1 %collective-permute-start.1 = (f32[64,1024]{1,0:T(8,128)S(1)}, f32[64,1024]{1,0:T(8,128)S(1)}, u32[]{:S(2)}, u32[]{:S(2)}) collective-permute-start(f32[64,1024]{1,0:T(8,128)S(1)} %convolution_add_fusion.4), channel_id=1, source_target_pairs={{0,32},{32,64},{64,96},{96,128},{128,160},{160,192},{192,224},{224... | collective-permute-start | bytes 786440 | tf_op jit(solution)/shard_map/while/body/eval_jaxpr/ppermute | solution.py:10
  154.2 19.1 %collective-permute-start = (bf16[64,1024]{1,0:T(8,128)(2,1)S(1)}, bf16[64,1024]{1,0:T(8,128)(2,1)S(1)}, u32[]{:S(2)}, u32[]{:S(2)}) collective-permute-start(bf16[64,1024]{1,0:T(8,128)(2,1)S(1)} %copy.12), channel_id=1, source_target_pairs={{0,32},{32,64},{64,96},{96,128},{128,160},{160,192},{192,224},{224... | collective-permute-start | bytes 393224 | tf_op jit(solution)/shard_map/while/body/eval_jaxpr/ppermute | solution.py:10
  166.5 17.0 %collective-permute-start.1 = (f32[64,1024]{1,0:T(8,128)S(1)}, f32[64,1024]{1,0:T(8,128)S(1)}, u32[]{:S(2)}, u32[]{:S(2)}) collective-permute-start(f32[64,1024]{1,0:T(8,128)S(1)} %convolution_add_fusion.4), channel_id=1, source_target_pairs={{0,32},{32,64},{64,96},{96,128},{128,160},{160,192},{192,224},{224... | collective-permute-start | bytes 786440 | tf_op jit(solution)/shard_map/while/body/eval_jaxpr/ppermute | solution.py:10
  183.5 14.2 %collective-permute-start = (bf16[64,1024]{1,0:T(8,128)(2,1)S(1)}, bf16[64,1024]{1,0:T(8,128)(2,1)S(1)}, u32[]{:S(2)}, u32[]{:S(2)}) collective-permute-start(bf16[64,1024]{1,0:T(8,128)(2,1)S(1)} %copy.12), channel_id=1, source_target_pairs={{0,32},{32,64},{64,96},{96,128},{128,160},{160,192},{192,224},{224... | collective-permute-start | bytes 393224 | tf_op jit(solution)/shard_map/while/body/eval_jaxpr/ppermute | solution.py:10
  190.8 18.4 %collective-permute-start.1 = (f32[64,1024]{1,0:T(8,128)S(1)}, f32[64,1024]{1,0:T(8,128)S(1)}, u32[]{:S(2)}, u32[]{:S(2)}) collective-permute-start(f32[64,1024]{1,0:T(8,128)S(1)} %convolution_add_fusion.4), channel_id=1, source_target_pairs={{0,32},{32,64},{64,96},{96,128},{128,160},{160,192},{192,224},{224... | collective-permute-start | bytes 786440 | tf_op jit(solution)/shard_map/while/body/eval_jaxpr/ppermute | solution.py:10
  209.2 17.2 %collective-permute-start = (bf16[64,1024]{1,0:T(8,128)(2,1)S(1)}, bf16[64,1024]{1,0:T(8,128)(2,1)S(1)}, u32[]{:S(2)}, u32[]{:S(2)}) collective-permute-start(bf16[64,1024]{1,0:T(8,128)(2,1)S(1)} %copy.12), channel_id=1, source_target_pairs={{0,32},{32,64},{64,96},{96,128},{128,160},{160,192},{192,224},{224... | collective-permute-start | bytes 393224 | tf_op jit(solution)/shard_map/while/body/eval_jaxpr/ppermute | solution.py:10
  215.4 17.8 %collective-permute-start.1 = (f32[64,1024]{1,0:T(8,128)S(1)}, f32[64,1024]{1,0:T(8,128)S(1)}, u32[]{:S(2)}, u32[]{:S(2)}) collective-permute-start(f32[64,1024]{1,0:T(8,128)S(1)} %convolution_add_fusion.4), channel_id=1, source_target_pairs={{0,32},{32,64},{64,96},{96,128},{128,160},{160,192},{192,224},{224... | collective-permute-start | bytes 786440 | tf_op jit(solution)/shard_map/while/body/eval_jaxpr/ppermute | solution.py:10
  233.2 13.1 %collective-permute-start = (bf16[64,1024]{1,0:T(8,128)(2,1)S(1)}, bf16[64,1024]{1,0:T(8,128)(2,1)S(1)}, u32[]{:S(2)}, u32[]{:S(2)}) collective-permute-start(bf16[64,1024]{1,0:T(8,128)(2,1)S(1)} %copy.12), channel_id=1, source_target_pairs={{0,32},{32,64},{64,96},{96,128},{128,160},{160,192},{192,224},{224... | collective-permute-start | bytes 393224 | tf_op jit(solution)/shard_map/while/body/eval_jaxpr/ppermute | solution.py:10
  238.2 18.2 %collective-permute-start.1 = (f32[64,1024]{1,0:T(8,128)S(1)}, f32[64,1024]{1,0:T(8,128)S(1)}, u32[]{:S(2)}, u32[]{:S(2)}) collective-permute-start(f32[64,1024]{1,0:T(8,128)S(1)} %convolution_add_fusion.4), channel_id=1, source_target_pairs={{0,32},{32,64},{64,96},{96,128},{128,160},{160,192},{192,224},{224... | collective-permute-start | bytes 786440 | tf_op jit(solution)/shard_map/while/body/eval_jaxpr/ppermute | solution.py:10
  256.4 18.5 %collective-permute-start = (bf16[64,1024]{1,0:T(8,128)(2,1)S(1)}, bf16[64,1024]{1,0:T(8,128)(2,1)S(1)}, u32[]{:S(2)}, u32[]{:S(2)}) collective-permute-start(bf16[64,1024]{1,0:T(8,128)(2,1)S(1)} %copy.12), channel_id=1, source_target_pairs={{0,32},{32,64},{64,96},{96,128},{128,160},{160,192},{192,224},{224... | collective-permute-start | bytes 393224 | tf_op jit(solution)/shard_map/while/body/eval_jaxpr/ppermute | solution.py:10
  266.1 16.9 %collective-permute-start.1 = (f32[64,1024]{1,0:T(8,128)S(1)}, f32[64,1024]{1,0:T(8,128)S(1)}, u32[]{:S(2)}, u32[]{:S(2)}) collective-permute-start(f32[64,1024]{1,0:T(8,128)S(1)} %convolution_add_fusion.4), channel_id=1, source_target_pairs={{0,32},{32,64},{64,96},{96,128},{128,160},{160,192},{192,224},{224... | collective-permute-start | bytes 786440 | tf_op jit(solution)/shard_map/while/body/eval_jaxpr/ppermute | solution.py:10
  283.1 18.2 %collective-permute-start = (bf16[64,1024]{1,0:T(8,128)(2,1)S(1)}, bf16[64,1024]{1,0:T(8,128)(2,1)S(1)}, u32[]{:S(2)}, u32[]{:S(2)}) collective-permute-start(bf16[64,1024]{1,0:T(8,128)(2,1)S(1)} %copy.12), channel_id=1, source_target_pairs={{0,32},{32,64},{64,96},{96,128},{128,160},{160,192},{192,224},{224... | collective-permute-start | bytes 393224 | tf_op jit(solution)/shard_map/while/body/eval_jaxpr/ppermute | solution.py:10
  295.3 18.8 %collective-permute-start.1 = (f32[64,1024]{1,0:T(8,128)S(1)}, f32[64,1024]{1,0:T(8,128)S(1)}, u32[]{:S(2)}, u32[]{:S(2)}) collective-permute-start(f32[64,1024]{1,0:T(8,128)S(1)} %convolution_add_fusion.4), channel_id=1, source_target_pairs={{0,32},{32,64},{64,96},{96,128},{128,160},{160,192},{192,224},{224... | collective-permute-start | bytes 786440 | tf_op jit(solution)/shard_map/while/body/eval_jaxpr/ppermute | solution.py:10
  314.1 16.2 %collective-permute-start = (bf16[64,1024]{1,0:T(8,128)(2,1)S(1)}, bf16[64,1024]{1,0:T(8,128)(2,1)S(1)}, u32[]{:S(2)}, u32[]{:S(2)}) collective-permute-start(bf16[64,1024]{1,0:T(8,128)(2,1)S(1)} %copy.12), channel_id=1, source_target_pairs={{0,32},{32,64},{64,96},{96,128},{128,160},{160,192},{192,224},{224... | collective-permute-start | bytes 393224 | tf_op jit(solution)/shard_map/while/body/eval_jaxpr/ppermute | solution.py:10
  321.6 20.4 %collective-permute-start.1 = (f32[64,1024]{1,0:T(8,128)S(1)}, f32[64,1024]{1,0:T(8,128)S(1)}, u32[]{:S(2)}, u32[]{:S(2)}) collective-permute-start(f32[64,1024]{1,0:T(8,128)S(1)} %convolution_add_fusion.4), channel_id=1, source_target_pairs={{0,32},{32,64},{64,96},{96,128},{128,160},{160,192},{192,224},{224... | collective-permute-start | bytes 786440 | tf_op jit(solution)/shard_map/while/body/eval_jaxpr/ppermute | solution.py:10
  342.0 13.8 %collective-permute-start = (bf16[64,1024]{1,0:T(8,128)(2,1)S(1)}, bf16[64,1024]{1,0:T(8,128)(2,1)S(1)}, u32[]{:S(2)}, u32[]{:S(2)}) collective-permute-start(bf16[64,1024]{1,0:T(8,128)(2,1)S(1)} %copy.12), channel_id=1, source_target_pairs={{0,32},{32,64},{64,96},{96,128},{128,160},{160,192},{192,224},{224... | collective-permute-start | bytes 393224 | tf_op jit(solution)/shard_map/while/body/eval_jaxpr/ppermute | solution.py:10
  353.0 17.9 %collective-permute-start.1 = (f32[64,1024]{1,0:T(8,128)S(1)}, f32[64,1024]{1,0:T(8,128)S(1)}, u32[]{:S(2)}, u32[]{:S(2)}) collective-permute-start(f32[64,1024]{1,0:T(8,128)S(1)} %convolution_add_fusion.4), channel_id=1, source_target_pairs={{0,32},{32,64},{64,96},{96,128},{128,160},{160,192},{192,224},{224... | collective-permute-start | bytes 786440 | tf_op jit(solution)/shard_map/while/body/eval_jaxpr/ppermute | solution.py:10
  370.9 20.1 %collective-permute-start = (bf16[64,1024]{1,0:T(8,128)(2,1)S(1)}, bf16[64,1024]{1,0:T(8,128)(2,1)S(1)}, u32[]{:S(2)}, u32[]{:S(2)}) collective-permute-start(bf16[64,1024]{1,0:T(8,128)(2,1)S(1)} %copy.12), channel_id=1, source_target_pairs={{0,32},{32,64},{64,96},{96,128},{128,160},{160,192},{192,224},{224... | collective-permute-start | bytes 393224 | tf_op jit(solution)/shard_map/while/body/eval_jaxpr/ppermute | solution.py:10
  375.9 19.9 %collective-permute-start.1 = (f32[64,1024]{1,0:T(8,128)S(1)}, f32[64,1024]{1,0:T(8,128)S(1)}, u32[]{:S(2)}, u32[]{:S(2)}) collective-permute-start(f32[64,1024]{1,0:T(8,128)S(1)} %convolution_add_fusion.4), channel_id=1, source_target_pairs={{0,32},{32,64},{64,96},{96,128},{128,160},{160,192},{192,224},{224... | collective-permute-start | bytes 786440 | tf_op jit(solution)/shard_map/while/body/eval_jaxpr/ppermute | solution.py:10
  395.8 13.6 %collective-permute-start = (bf16[64,1024]{1,0:T(8,128)(2,1)S(1)}, bf16[64,1024]{1,0:T(8,128)(2,1)S(1)}, u32[]{:S(2)}, u32[]{:S(2)}) collective-permute-start(bf16[64,1024]{1,0:T(8,128)(2,1)S(1)} %copy.12), channel_id=1, source_target_pairs={{0,32},{32,64},{64,96},{96,128},{128,160},{160,192},{192,224},{224... | collective-permute-start | bytes 393224 | tf_op jit(solution)/shard_map/while/body/eval_jaxpr/ppermute | solution.py:10
  400.7 16.9 %collective-permute-start.1 = (f32[64,1024]{1,0:T(8,128)S(1)}, f32[64,1024]{1,0:T(8,128)S(1)}, u32[]{:S(2)}, u32[]{:S(2)}) collective-permute-start(f32[64,1024]{1,0:T(8,128)S(1)} %convolution_add_fusion.4), channel_id=1, source_target_pairs={{0,32},{32,64},{64,96},{96,128},{128,160},{160,192},{192,224},{224... | collective-permute-start | bytes 786440 | tf_op jit(solution)/shard_map/while/body/eval_jaxpr/ppermute | solution.py:10
  417.6 13.4 %collective-permute-start = (bf16[64,1024]{1,0:T(8,128)(2,1)S(1)}, bf16[64,1024]{1,0:T(8,128)(2,1)S(1)}, u32[]{:S(2)}, u32[]{:S(2)}) collective-permute-start(bf16[64,1024]{1,0:T(8,128)(2,1)S(1)} %copy.12), channel_id=1, source_target_pairs={{0,32},{32,64},{64,96},{96,128},{128,160},{160,192},{192,224},{224... | collective-permute-start | bytes 393224 | tf_op jit(solution)/shard_map/while/body/eval_jaxpr/ppermute | solution.py:10
  422.6 18.1 %collective-permute-start.1 = (f32[64,1024]{1,0:T(8,128)S(1)}, f32[64,1024]{1,0:T(8,128)S(1)}, u32[]{:S(2)}, u32[]{:S(2)}) collective-permute-start(f32[64,1024]{1,0:T(8,128)S(1)} %convolution_add_fusion.4), channel_id=1, source_target_pairs={{0,32},{32,64},{64,96},{96,128},{128,160},{160,192},{192,224},{224... | collective-permute-start | bytes 786440 | tf_op jit(solution)/shard_map/while/body/eval_jaxpr/ppermute | solution.py:10
  440.7 14.2 %collective-permute-start = (bf16[64,1024]{1,0:T(8,128)(2,1)S(1)}, bf16[64,1024]{1,0:T(8,128)(2,1)S(1)}, u32[]{:S(2)}, u32[]{:S(2)}) collective-permute-start(bf16[64,1024]{1,0:T(8,128)(2,1)S(1)} %copy.12), channel_id=1, source_target_pairs={{0,32},{32,64},{64,96},{96,128},{128,160},{160,192},{192,224},{224... | collective-permute-start | bytes 393224 | tf_op jit(solution)/shard_map/while/body/eval_jaxpr/ppermute | solution.py:10
  448.0 17.4 %collective-permute-start.1 = (f32[64,1024]{1,0:T(8,128)S(1)}, f32[64,1024]{1,0:T(8,128)S(1)}, u32[]{:S(2)}, u32[]{:S(2)}) collective-permute-start(f32[64,1024]{1,0:T(8,128)S(1)} %convolution_add_fusion.4), channel_id=1, source_target_pairs={{0,32},{32,64},{64,96},{96,128},{128,160},{160,192},{192,224},{224... | collective-permute-start | bytes 786440 | tf_op jit(solution)/shard_map/while/body/eval_jaxpr/ppermute | solution.py:10
  465.4 16.2 %collective-permute-start = (bf16[64,1024]{1,0:T(8,128)(2,1)S(1)}, bf16[64,1024]{1,0:T(8,128)(2,1)S(1)}, u32[]{:S(2)}, u32[]{:S(2)}) collective-permute-start(bf16[64,1024]{1,0:T(8,128)(2,1)S(1)} %copy.12), channel_id=1, source_target_pairs={{0,32},{32,64},{64,96},{96,128},{128,160},{160,192},{192,224},{224... | collective-permute-start | bytes 393224 | tf_op jit(solution)/shard_map/while/body/eval_jaxpr/ppermute | solution.py:10
  474.0 21.2 %collective-permute-start.1 = (f32[64,1024]{1,0:T(8,128)S(1)}, f32[64,1024]{1,0:T(8,128)S(1)}, u32[]{:S(2)}, u32[]{:S(2)}) collective-permute-start(f32[64,1024]{1,0:T(8,128)S(1)} %convolution_add_fusion.4), channel_id=1, source_target_pairs={{0,32},{32,64},{64,96},{96,128},{128,160},{160,192},{192,224},{224... | collective-permute-start | bytes 786440 | tf_op jit(solution)/shard_map/while/body/eval_jaxpr/ppermute | solution.py:10
  495.2 20.2 %collective-permute-start = (bf16[64,1024]{1,0:T(8,128)(2,1)S(1)}, bf16[64,1024]{1,0:T(8,128)(2,1)S(1)}, u32[]{:S(2)}, u32[]{:S(2)}) collective-permute-start(bf16[64,1024]{1,0:T(8,128)(2,1)S(1)} %copy.12), channel_id=1, source_target_pairs={{0,32},{32,64},{64,96},{96,128},{128,160},{160,192},{192,224},{224... | collective-permute-start | bytes 393224 | tf_op jit(solution)/shard_map/while/body/eval_jaxpr/ppermute | solution.py:10
  501.3 20.3 %collective-permute-start.1 = (f32[64,1024]{1,0:T(8,128)S(1)}, f32[64,1024]{1,0:T(8,128)S(1)}, u32[]{:S(2)}, u32[]{:S(2)}) collective-permute-start(f32[64,1024]{1,0:T(8,128)S(1)} %convolution_add_fusion.4), channel_id=1, source_target_pairs={{0,32},{32,64},{64,96},{96,128},{128,160},{160,192},{192,224},{224... | collective-permute-start | bytes 786440 | tf_op jit(solution)/shard_map/while/body/eval_jaxpr/ppermute | solution.py:10
  521.6 16.1 %collective-permute-start = (bf16[64,1024]{1,0:T(8,128)(2,1)S(1)}, bf16[64,1024]{1,0:T(8,128)(2,1)S(1)}, u32[]{:S(2)}, u32[]{:S(2)}) collective-permute-start(bf16[64,1024]{1,0:T(8,128)(2,1)S(1)} %copy.12), channel_id=1, source_target_pairs={{0,32},{32,64},{64,96},{96,128},{128,160},{160,192},{192,224},{224... | collective-permute-start | bytes 393224 | tf_op jit(solution)/shard_map/while/body/eval_jaxpr/ppermute | solution.py:10
  526.5 18.7 %collective-permute-start.1 = (f32[64,1024]{1,0:T(8,128)S(1)}, f32[64,1024]{1,0:T(8,128)S(1)}, u32[]{:S(2)}, u32[]{:S(2)}) collective-permute-start(f32[64,1024]{1,0:T(8,128)S(1)} %convolution_add_fusion.4), channel_id=1, source_target_pairs={{0,32},{32,64},{64,96},{96,128},{128,160},{160,192},{192,224},{224... | collective-permute-start | bytes 786440 | tf_op jit(solution)/shard_map/while/body/eval_jaxpr/ppermute | solution.py:10
  545.2 17.7 %collective-permute-start = (bf16[64,1024]{1,0:T(8,128)(2,1)S(1)}, bf16[64,1024]{1,0:T(8,128)(2,1)S(1)}, u32[]{:S(2)}, u32[]{:S(2)}) collective-permute-start(bf16[64,1024]{1,0:T(8,128)(2,1)S(1)} %copy.12), channel_id=1, source_target_pairs={{0,32},{32,64},{64,96},{96,128},{128,160},{160,192},{192,224},{224... | collective-permute-start | bytes 393224 | tf_op jit(solution)/shard_map/while/body/eval_jaxpr/ppermute | solution.py:10
  550.1 19.7 %collective-permute-start.1 = (f32[64,1024]{1,0:T(8,128)S(1)}, f32[64,1024]{1,0:T(8,128)S(1)}, u32[]{:S(2)}, u32[]{:S(2)}) collective-permute-start(f32[64,1024]{1,0:T(8,128)S(1)} %convolution_add_fusion.4), channel_id=1, source_target_pairs={{0,32},{32,64},{64,96},{96,128},{128,160},{160,192},{192,224},{224... | collective-permute-start | bytes 786440 | tf_op jit(solution)/shard_map/while/body/eval_jaxpr/ppermute | solution.py:10
  574.8 16.8 %collective-permute-start.1 = (f32[64,1024]{1,0:T(8,128)S(1)}, f32[64,1024]{1,0:T(8,128)S(1)}, u32[]{:S(2)}, u32[]{:S(2)}) collective-permute-start(f32[64,1024]{1,0:T(8,128)S(1)} %convolution_add_fusion.4), channel_id=1, source_target_pairs={{0,32},{32,64},{64,96},{96,128},{128,160},{160,192},{192,224},{224... | collective-permute-start | bytes 786440 | tf_op jit(solution)/shard_map/while/body/eval_jaxpr/ppermute | solution.py:10
  591.6 20.5 %collective-permute-start = (bf16[64,1024]{1,0:T(8,128)(2,1)S(1)}, bf16[64,1024]{1,0:T(8,128)(2,1)S(1)}, u32[]{:S(2)}, u32[]{:S(2)}) collective-permute-start(bf16[64,1024]{1,0:T(8,128)(2,1)S(1)} %copy.12), channel_id=1, source_target_pairs={{0,32},{32,64},{64,96},{96,128},{128,160},{160,192},{192,224},{224... | collective-permute-start | bytes 393224 | tf_op jit(solution)/shard_map/while/body/eval_jaxpr/ppermute | solution.py:10
  603.4 15.4 %collective-permute-start.1 = (f32[64,1024]{1,0:T(8,128)S(1)}, f32[64,1024]{1,0:T(8,128)S(1)}, u32[]{:S(2)}, u32[]{:S(2)}) collective-permute-start(f32[64,1024]{1,0:T(8,128)S(1)} %convolution_add_fusion.4), channel_id=1, source_target_pairs={{0,32},{32,64},{64,96},{96,128},{128,160},{160,192},{192,224},{224... | collective-permute-start | bytes 786440 | tf_op jit(solution)/shard_map/while/body/eval_jaxpr/ppermute | solution.py:10
  618.8 15.0 %collective-permute-start = (bf16[64,1024]{1,0:T(8,128)(2,1)S(1)}, bf16[64,1024]{1,0:T(8,128)(2,1)S(1)}, u32[]{:S(2)}, u32[]{:S(2)}) collective-permute-start(bf16[64,1024]{1,0:T(8,128)(2,1)S(1)} %copy.12), channel_id=1, source_target_pairs={{0,32},{32,64},{64,96},{96,128},{128,160},{160,192},{192,224},{224... | collective-permute-start | bytes 393224 | tf_op jit(solution)/shard_map/while/body/eval_jaxpr/ppermute | solution.py:10
  631.5 15.0 %collective-permute-start.1 = (f32[64,1024]{1,0:T(8,128)S(1)}, f32[64,1024]{1,0:T(8,128)S(1)}, u32[]{:S(2)}, u32[]{:S(2)}) collective-permute-start(f32[64,1024]{1,0:T(8,128)S(1)} %convolution_add_fusion.4), channel_id=1, source_target_pairs={{0,32},{32,64},{64,96},{96,128},{128,160},{160,192},{192,224},{224... | collective-permute-start | bytes 786440 | tf_op jit(solution)/shard_map/while/body/eval_jaxpr/ppermute | solution.py:10
  (4 other events, 14.5 us)
where the time goes:
time: 650 us; the launch traced here: 648 us
  waiting for transfers between devices  318 us (49%)
  starting transfers between devices  245 us (38%)
  matrix products  52.8 us (8%)
  local copies, waits for them, and re-layouts  16.2 us (2%)
  loops' own time  15.4 us (2%)
    ppermute x48, waiting for transfers between devices, shifted_2(): return lax.ppermute(value, axis, pairs)  302 us
    ppermute x48, starting transfers between devices, shifted_2(): return lax.ppermute(value, axis, pairs)  239 us
    dot_general x24, matrix products, cycle_step(): lax.dot_general(cov_piece, panel, (((1,), (1,)), ((), ())), preferred_ele...  38.4 us
    another operation x1, loops' own time, local(): lax.scan(cycle_step, (cov_own, start_sum, start_text), jnp.arange(cycle_l...  15.4 us
    all_to_all x1, waiting for transfers between devices, local(): lax.all_to_all(text_emb, 'section', split_axis=0, concat_axis=1, tiled=True)  15.4 us
    dynamic_slice x24, local copies, waits for them, and re-layouts, local(): lax.scan(cycle_step, (cov_own, start_sum, start_text), jnp.arange(cycle_l...  14 us
  transfers between devices with their start and end apart: 49, of which 37 were waited for; matrix products, arithmetic and copies ran while one was open for 10% of the time, Pallas kernels for 0%

commit v1 on v0

v1 whole, which is shorter than its diff:
```python
import functools

import jax
import jax.numpy as jnp
from jax import lax
from jax.experimental import pallas as pl
from jax.experimental.pallas import tpu as pltpu
from jax.sharding import PartitionSpec as P

MESH = pl.DeviceIdType.MESH
F32 = jnp.float32
BF16 = jnp.bfloat16
PIECES = 4
Y_LO = 4


def kernel(
    dims,
    panel_ref, cov_ref, lab_ref, scale_ref, bias_ref,
    text_out, cov_out,
    cov_all, lab_far, weights, cov_part,
    rs_out, rs_in, last_out, last_in, tx_out, tx_mid, tx_in,
    ag_send, ag_recv, rs_send, rs_recv, t1_send, t1_recv, t2_send, t2_recv, lab_sem, own_sem,
):
    n_z, y_lo, per_y = dims
    reach = n_z // 2
    rows_dev, width = cov_ref.shape
    half_rows = rows_dev // 2
    blk, sec = lax.axis_index("blk"), lax.axis_index("section")
    z, y_hi = blk // 2, blk % 2
    y, rest = y_hi * y_lo + sec // per_y, sec % per_y

    def at_z(step):
        return {"blk": ((z + step + n_z) % n_z) * 2 + y_hi, "section": sec}

    def at_y(step):
        other = (y + step + 2 * y_lo) % (2 * y_lo)
        return {"blk": z * 2 + other // y_lo, "section": (other % y_lo) * per_y + rest}

    z_next = (at_z(1), at_z(-1))
    y_next = (at_y(y_lo // 2), at_y(-(y_lo // 2)))
    far = at_y(y_lo)

    barrier = pltpu.get_barrier_semaphore()
    for peer in (*z_next, *y_next, far):
        pl.semaphore_signal(barrier, inc=1, device_id=peer, device_id_type=MESH)
    pl.semaphore_wait(barrier, 5)

    def remote(src, dst, send, recv, peer):
        return pltpu.make_async_remote_copy(
            src_ref=src, dst_ref=dst, send_sem=send, recv_sem=recv, device_id=peer, device_id_type=MESH
        )

    lab_copy = remote(lab_ref, lab_far, lab_sem.at[0], lab_sem.at[1], far)
    lab_copy.start()

    def hops(way, half):
        return reach - (1 if way == half else 0) if n_z % 2 == 0 else reach

    def slot(way, k):
        return (k if way == 0 else -k) % n_z

    def gather_copy(way, half, k):
        src = cov_ref.at[pl.ds(half * half_rows, half_rows)] if k == 0 else cov_all.at[slot(way, k), half]
        return remote(
            src, cov_all.at[slot(way, k + 1), half],
            ag_send.at[way, half, k], ag_recv.at[way, half, k], z_next[way],
        )

    own_copies = [
        pltpu.make_async_copy(cov_ref.at[pl.ds(half * half_rows, half_rows)], cov_all.at[0, half], own_sem.at[half])
        for half in range(2)
    ]
    for k in range(reach):
        for half in range(2):
            for way in range(2):
                if k >= 1 and k - 1 < hops(way, half):
                    gather_copy(way, half, k - 1).wait_recv()
                if k < hops(way, half):
                    gather_copy(way, half, k).start()
    for copy in own_copies:
        copy.start()
    for copy in own_copies:
        copy.wait()
    for half in range(2):
        for way in range(2):
            if hops(way, half) == reach:
                gather_copy(way, half, reach - 1).wait_recv()
    lab_copy.wait_recv()

    scale, bias = scale_ref[0], bias_ref[0]
    rows_txt = lab_ref.shape[1]
    cov_rows = cov_all[...].reshape(n_z * rows_dev, width)
    row_at = lax.broadcasted_iota(jnp.int32, (rows_dev, rows_txt), 0)

    def panel_of(side):
        n_src = panel_ref.shape[0] // 2
        return panel_ref[pl.ds(side * n_src, n_src)].reshape(rows_txt, width)

    def fill_weights(panel, labels, column):
        logits = lax.dot_general(cov_rows, panel, (((1,), (1,)), ((), ())), preferred_element_type=F32)
        for k in range(n_z):
            part = logits[k * rows_dev : (k + 1) * rows_dev]
            first = (((z - k + n_z) % n_z) * 2 + y_hi) * rows_dev
            positive = (labels - first == row_at).astype(F32)
            value = scale * (jax.nn.sigmoid(scale * part + bias) - positive)
            weights[pl.ds(k * rows_dev, rows_dev), pl.ds(column, rows_txt)] = value.astype(BF16)

    def text_term(column):
        return lax.dot_general(
            weights[:, pl.ds(column, rows_txt)], cov_rows, (((0,), (0,)), ((), ())), preferred_element_type=F32
        )

    panel_far = panel_of(1 - y_hi)
    fill_weights(panel_far, lab_far[...], rows_txt)
    piece = rows_txt // (2 * PIECES)
    tx_out[...] = text_term(rows_txt).astype(BF16).reshape(2, PIECES, piece, width)

    def first_leg(way, j):
        return remote(
            tx_out.at[way, j], tx_mid.at[way, j], t1_send.at[way, j], t1_recv.at[way, j], y_next[way]
        )

    def second_leg(way, j):
        return remote(
            tx_mid.at[way, j], tx_in.at[way, j], t2_send.at[way, j], t2_recv.at[way, j], y_next[way]
        )

    for j in range(PIECES):
        for way in range(2):
            first_leg(way, j).start()

    panel_own = panel_of(y_hi)
    fill_weights(panel_own, lab_ref[...], 0)
    cov_part[...] = (
        jnp.dot(weights[:, pl.ds(0, rows_txt)], panel_own, preferred_element_type=F32)
        + jnp.dot(weights[:, pl.ds(rows_txt, rows_txt)], panel_far, preferred_element_type=F32)
    ).reshape(n_z, 2, half_rows, width)

    def part_of(way, half, m):
        return cov_part[(-m if way == 0 else m) % n_z, half]

    def sum_copy(way, half, m):
        src = last_out.at[way, half] if m == 1 else rs_out.at[way, half, m - 1]
        dst = last_in.at[way, half] if m == 1 else rs_in.at[way, half, m - 1]
        return remote(
            src, dst,
            rs_send.at[way, half, m - 1], rs_recv.at[way, half, m - 1], z_next[way],
        )

    def sum_start(way, half, m):
        total = part_of(way, half, m)
        if m < hops(way, half):
            sum_copy(way, half, m + 1).wait_recv()
            total = total + rs_in[way, half, m].astype(F32)
        if m == 1:
            last_out[way, half] = total
        else:
            rs_out[way, half, m - 1] = total.astype(BF16)
        sum_copy(way, half, m).start()

    for half in range(2):
        for way in range(2):
            sum_start(way, half, hops(way, half))
    text_out[...] = text_term(0)

    forwarded = 0
    for step in range(1, reach):
        if forwarded < PIECES:
            for way in range(2):
                first_leg(way, forwarded).wait_recv()
                second_leg(way, forwarded).start()
            forwarded += 1
        for half in range(2):
            for way in range(2):
                m = hops(way, half) - step
                if m >= 1:
                    sum_start(way, half, m)
    while forwarded < PIECES:
        for way in range(2):
            first_leg(way, forwarded).wait_recv()
            second_leg(way, forwarded).start()
        forwarded += 1

    for half in range(2):
        total = cov_part[0, half]
        for way in range(2):
            sum_copy(way, half, 1).wait_recv()
            total = total + last_in[way, half]
        cov_out[pl.ds(half * half_rows, half_rows)] = total

    for j in range(PIECES):
        for way in range(2):
            second_leg(way, j).wait_recv()
            rows = pl.ds((way * PIECES + j) * piece, piece)
            text_out[rows] = text_out[rows] + tx_in[way, j].astype(F32)

    lab_copy.wait_send()
    for half in range(2):
        for way in range(2):
            for k in range(hops(way, half)):
                gather_copy(way, half, k).wait_send()
                sum_copy(way, half, k + 1).wait_send()
    for j in range(PIECES):
        for way in range(2):
            first_leg(way, j).wait_send()
            second_leg(way, j).wait_send()


def local(dims, text_emb, covariate, labels, logit_scale, logit_bias):
    n_z, y_lo, per_y = dims
    sections = y_lo * per_y
    plane = 2 * sections
    groups = [[at * plane + i for i in range(plane)] for at in range(n_z)]
    panel = lax.all_to_all(
        jnp.concatenate([text_emb, text_emb], 0), ("blk", "section"),
        split_axis=0, concat_axis=0, tiled=True, axis_index_groups=groups,
    )
    cov_own = covariate[0]
    rows_dev, width = cov_own.shape
    rows_txt = labels.shape[1]
    piece = rows_txt // (2 * PIECES)
    reach = n_z // 2
    half_rows = rows_dev // 2
    dma = pltpu.SemaphoreType.DMA
    vmem = pl.BlockSpec(memory_space=pltpu.VMEM)
    smem = pl.BlockSpec(memory_space=pltpu.SMEM)
    text_grad, cov_grad = pl.pallas_call(
        functools.partial(kernel, dims),
        out_shape=(
            jax.ShapeDtypeStruct((rows_txt, width), F32),
            jax.ShapeDtypeStruct((rows_dev, width), F32),
        ),
        in_specs=[vmem, vmem, vmem, smem, smem],
        out_specs=(vmem, vmem),
        scratch_shapes=[
            pltpu.VMEM((n_z, 2, half_rows, width), BF16),
            pltpu.VMEM((1, rows_txt), jnp.int32),
            pltpu.VMEM((n_z * rows_dev, 2 * rows_txt), BF16),
            pltpu.VMEM((n_z, 2, half_rows, width), F32),
            pltpu.VMEM((2, 2, reach, half_rows, width), BF16),
            pltpu.VMEM((2, 2, reach, half_rows, width), BF16),
            pltpu.VMEM((2, 2, half_rows, width), F32),
            pltpu.VMEM((2, 2, half_rows, width), F32),
            pltpu.VMEM((2, PIECES, piece, width), BF16),
            pltpu.VMEM((2, PIECES, piece, width), BF16),
            pltpu.VMEM((2, PIECES, piece, width), BF16),
            dma((2, 2, reach)), dma((2, 2, reach)), dma((2, 2, reach)), dma((2, 2, reach)),
            dma((2, PIECES)), dma((2, PIECES)), dma((2, PIECES)), dma((2, PIECES)),
            dma((2,)), dma((2,)),
        ],
        compiler_params=pltpu.CompilerParams(
            collective_id=0, has_side_effects=True, vmem_limit_bytes=48 * 1024 * 1024
        ),
    )(panel, cov_own, labels, logit_scale, logit_bias)
    return text_grad[None], cov_grad[None]


def solution(mesh):
    dims = (mesh.shape["blk"] // 2, Y_LO, mesh.shape["section"] // Y_LO)
    return jax.shard_map(
        functools.partial(local, dims),
        mesh=mesh,
        in_specs=(
            P(None, ("blk", "section"), None),
            P("section", "blk", None),
            P("section", "blk"),
            P(),
            P(),
        ),
        out_specs=(P("section", "blk", None), P("section", "blk", None)),
        check_vma=False,
    )
```

time: 650 us -> 115 us (0.18)
  the two profiles are of different devices: /device:TPU:104 before, /device:TPU:6 now
where the time goes in v1:
time: 115 us
  Pallas kernels  67.7 us (59%)
  waiting for transfers between devices  27.6 us (24%)
  starting transfers between devices  13.7 us (12%)
  other arithmetic  2.26 us (2%)
  between operations  1.95 us (2%)
  local copies, waits for them, and re-layouts  1.68 us (1%)
    pallas_call x1, Pallas kernels, local(): pl.pallas_call(functools.partial(kernel, dims), out_shape=(jax.ShapeDtype...  67.7 us
    all_to_all x1, waiting for transfers between devices, local(): lax.all_to_all(jnp.concatenate([text_emb, text_emb], 0), ('blk', 'section...  27.6 us
    all_to_all x1, starting transfers between devices, local(): lax.all_to_all(jnp.concatenate([text_emb, text_emb], 0), ('blk', 'section...  13.7 us
  transfers between devices with their start and end apart: 1, of which 1 were waited for; matrix products, arithmetic and copies ran while one was open for 0% of the time, Pallas kernels for 0%

profile of v1, /device:TPU:6, one launch (start us, length us, event | category | flops | bytes accessed | tf_op | source)
XLA Modules:
  0.0 114.9 jit_solution(10681715727355817276)
XLA Ops:
  0.6 2.3 %pad_maximum_fusion = bf16[64,8,1024]{2,1,0:T(8,128)(2,1)} fusion(bf16[32,8,1024]{2,1,0:T(8,128)(2,1)} %param.5), kind=kLoop, calls=%fused_computation | loop fusion | flops 524288 | bytes 1572864 | tf_op jit(solution)/shard_map/concatenate | solution.py:216
  2.9 0.0 copy-start
  2.9 13.7 %all-to-all-start = ((bf16[64,8,1024]{2,1,0:T(8,128)(2,1)}), bf16[64,8,1024]{2,1,0:T(8,128)(2,1)S(1)}, u32[]{:S(2)}, u32[]{:S(2)}) async-start(bf16[64,8,1024]{2,1,0:T(8,128)(2,1)} %pad_maximum_fusion), calls=%async_computation | async-start | bytes 2097152 | tf_op jit(solution)/shard_map/all_to_all | solution.py:215
  17.9 0.0 copy-start.1
  17.9 27.6 %all-to-all-done.panel_ref = bf16[64,8,1024]{2,1,0:T(8,128)(2,1)S(1)} async-done(((bf16[64,8,1024]{2,1,0:T(8,128)(2,1)}), bf16[64,8,1024]{2,1,0:T(8,128)(2,1)S(1)}, u32[]{:S(2)}, u32[]{:S(2)}) %all-to-all-start) | async-done | bytes 1048608 | tf_op jit(solution)/shard_map/all_to_all | solution.py:215
  45.5 0.0 copy-done
  45.5 0.0 copy-done.1
  45.5 67.7 %shard_map.68 = (f32[256,1024]{1,0:T(8,128)S(1)}, f32[64,1024]{1,0:T(8,128)S(1)}) custom-call(bf16[64,8,1024]{2,1,0:T(8,128)(2,1)S(1)} %all-to-all-done.panel_ref, bf16[64,1024]{1,0:T(8,128)(2,1)S(1)} %bitcast.5, s32[1,256]{1,0:T(1,128)S(1)} %copy-done.1, f32[1]{0:T(128)S(6)} %copy.9.scale_ref, f32[1]{0:T(128)S(6)} %copy.10.bias_ref), custom_call_target="tpu_custom_call" | custom-call | tf_op jit(solution)/shard_map/pallas_call | solution.py:228
  113.2 1.0 copy.11
  114.2 0.7 copy.12
Async XLA Ops:
  2.9 42.6 %copy-start = (bf16[1,64,1024]{2,1,0:T(8,128)(2,1)S(1)}, bf16[1,64,1024]{2,1,0:T(8,128)(2,1)}, u32[]{:S(2)}) copy-start(bf16[1,64,1024]{2,1,0:T(8,128)(2,1)} %param.6) | copy-start | bytes 393220
  2.9 42.6 %all-to-all-start = ((bf16[64,8,1024]{2,1,0:T(8,128)(2,1)}), bf16[64,8,1024]{2,1,0:T(8,128)(2,1)S(1)}, u32[]{:S(2)}, u32[]{:S(2)}) async-start(bf16[64,8,1024]{2,1,0:T(8,128)(2,1)} %pad_maximum_fusion), calls=%async_computation | async-start | bytes 2097152 | tf_op jit(solution)/shard_map/all_to_all | solution.py:215
  17.9 27.6 %copy-start.1 = (s32[1,256]{1,0:T(1,128)S(1)}, s32[1,256]{1,0:T(1,128)}, u32[]{:S(2)}) copy-start(s32[1,256]{1,0:T(1,128)} %lab_ref.1) | copy-start | bytes 3076

commit v2 on v1

--- a/solution.py
+++ b/solution.py
@@ -10,17 +10,19 @@
 MESH = pl.DeviceIdType.MESH
 F32 = jnp.float32
 BF16 = jnp.bfloat16
-PIECES = 4
+PIECES = 8
+TIE_RELAY = True
 Y_LO = 4
 
 
 def kernel(
     dims,
-    panel_ref, cov_ref, lab_ref, scale_ref, bias_ref,
+    text_ref, cov_ref, lab_ref, scale_ref, bias_ref,
     text_out, cov_out,
-    cov_all, lab_far, weights, cov_part,
+    panel, tie_buf, cov_all, lab_far, weights, cov_part,
     rs_out, rs_in, last_out, last_in, tx_out, tx_mid, tx_in,
     ag_send, ag_recv, rs_send, rs_recv, t1_send, t1_recv, t2_send, t2_recv, lab_sem, own_sem,
+    near_sem, far_sem, tie_send, tie_recv, tie_out,
 ):
     n_z, y_lo, per_y = dims
     reach = n_z // 2
@@ -41,15 +43,56 @@
     y_next = (at_y(y_lo // 2), at_y(-(y_lo // 2)))
     far = at_y(y_lo)
 
+    sections = y_lo * per_y
+    plane = 2 * sections
     barrier = pltpu.get_barrier_semaphore()
-    for peer in (*z_next, *y_next, far):
+    for peer in z_next:
         pl.semaphore_signal(barrier, inc=1, device_id=peer, device_id_type=MESH)
-    pl.semaphore_wait(barrier, 5)
+
+    @pl.loop(1, plane)
+    def _(step):
+        other = (y_hi * sections + sec + step) % plane
+        peer = {"blk": z * 2 + other // sections, "section": other % sections}
+        pl.semaphore_signal(barrier, inc=1, device_id=peer, device_id_type=MESH)
+
+    pl.semaphore_wait(barrier, plane + 1)
 
     def remote(src, dst, send, recv, peer):
         return pltpu.make_async_remote_copy(
             src_ref=src, dst_ref=dst, send_sem=send, recv_sem=recv, device_id=peer, device_id_type=MESH
         )
+
+    near_send, near_recv, far_send, far_recv = near_sem.at[0], near_sem.at[1], far_sem.at[0], far_sem.at[1]
+    half_y = per_y // 2
+    y_own = sec // per_y
+
+    def tie_copy(way):
+        return remote(
+            text_ref.at[pl.ds(y_own * per_y + way * half_y, half_y)], tie_buf.at[way],
+            tie_send.at[way], tie_recv.at[way], y_next[way],
+        )
+
+    def tie_onward(way):
+        y_from = (y + (-1 if way == 0 else 1) * (y_lo // 2) + 2 * y_lo) % (2 * y_lo)
+        y_to = (y + (1 if way == 0 else -1) * (y_lo // 2) + 2 * y_lo) % (2 * y_lo)
+        origin = (y_from % y_lo) * per_y + rest
+
+        @pl.loop(0, half_y)
+        def _(i):
+            peer = {"blk": z * 2 + y_to // y_lo, "section": (y_to % y_lo) * per_y + way * half_y + i}
+            remote(tie_buf.at[way, i], panel.at[1, origin], tie_out.at[way], far_recv, peer).start()
+
+    if TIE_RELAY:
+        for way in range(2):
+            tie_copy(way).start()
+
+    @pl.loop(0, per_y)
+    def _(step):
+        column = (rest + step) % per_y
+        for dy in range(1 if TIE_RELAY else 0, y_lo):
+            to = ((y_own + dy) % y_lo) * per_y + column
+            peer = {"blk": z * 2 + 1 - y_hi, "section": to}
+            remote(text_ref.at[to], panel.at[1, sec], far_send, far_recv, peer).start()
 
     lab_copy = remote(lab_ref, lab_far, lab_sem.at[0], lab_sem.at[1], far)
     lab_copy.start()
@@ -72,6 +115,27 @@
         for half in range(2)
     ]
     for k in range(reach):
+        if k == 1:
+
+            @pl.loop(0, per_y)
+            def _(step):
+                column = (rest + step) % per_y
+                for dy in range(1, y_lo):
+                    to = ((y_own + dy) % y_lo) * per_y + column
+                    peer = {"blk": blk, "section": to}
+                    remote(text_ref.at[to], panel.at[0, sec], near_send, near_recv, peer).start()
+
+            @pl.loop(1, per_y)
+            def _(step):
+                to = y_own * per_y + (rest + step) % per_y
+                peer = {"blk": blk, "section": to}
+                remote(text_ref.at[to], panel.at[0, sec], near_send, near_recv, peer).start()
+
+            pltpu.make_async_copy(text_ref.at[sec], panel.at[0, sec], near_recv).start()
+        if k == min(2, reach - 1) and TIE_RELAY:
+            for way in range(2):
+                tie_copy(way).wait_recv()
+                tie_onward(way)
         for half in range(2):
             for way in range(2):
                 if k >= 1 and k - 1 < hops(way, half):
@@ -93,9 +157,8 @@
     cov_rows = cov_all[...].reshape(n_z * rows_dev, width)
     row_at = lax.broadcasted_iota(jnp.int32, (rows_dev, rows_txt), 0)
 
-    def panel_of(side):
-        n_src = panel_ref.shape[0] // 2
-        return panel_ref[pl.ds(side * n_src, n_src)].reshape(rows_txt, width)
+    def whole(side, send, recv):
+        return remote(panel.at[side], panel.at[side], send, recv, far)
 
     def fill_weights(panel, labels, column):
         logits = lax.dot_general(cov_rows, panel, (((1,), (1,)), ((), ())), preferred_element_type=F32)
@@ -111,7 +174,8 @@
             weights[:, pl.ds(column, rows_txt)], cov_rows, (((0,), (0,)), ((), ())), preferred_element_type=F32
         )
 
-    panel_far = panel_of(1 - y_hi)
+    whole(1, far_send, far_recv).wait_recv()
+    panel_far = panel[1].reshape(rows_txt, width)
     fill_weights(panel_far, lab_far[...], rows_txt)
     piece = rows_txt // (2 * PIECES)
     tx_out[...] = text_term(rows_txt).astype(BF16).reshape(2, PIECES, piece, width)
@@ -130,7 +194,8 @@
         for way in range(2):
             first_leg(way, j).start()
 
-    panel_own = panel_of(y_hi)
+    whole(0, near_send, near_recv).wait_recv()
+    panel_own = panel[0].reshape(rows_txt, width)
     fill_weights(panel_own, lab_ref[...], 0)
     cov_part[...] = (
         jnp.dot(weights[:, pl.ds(0, rows_txt)], panel_own, preferred_element_type=F32)
@@ -164,23 +229,23 @@
             sum_start(way, half, hops(way, half))
     text_out[...] = text_term(0)
 
+    def forward(j):
+        for way in range(2):
+            first_leg(way, j).wait_recv()
+            second_leg(way, j).start()
+
     forwarded = 0
     for step in range(1, reach):
-        if forwarded < PIECES:
-            for way in range(2):
-                first_leg(way, forwarded).wait_recv()
-                second_leg(way, forwarded).start()
-            forwarded += 1
         for half in range(2):
+            if forwarded < PIECES:
+                forward(forwarded)
+                forwarded += 1
             for way in range(2):
                 m = hops(way, half) - step
                 if m >= 1:
                     sum_start(way, half, m)
-    while forwarded < PIECES:
-        for way in range(2):
-            first_leg(way, forwarded).wait_recv()
-            second_leg(way, forwarded).start()
-        forwarded += 1
+    for j in range(forwarded, PIECES):
+        forward(j)
 
     for half in range(2):
         total = cov_part[0, half]
@@ -196,6 +261,14 @@
             text_out[rows] = text_out[rows] + tx_in[way, j].astype(F32)
 
     lab_copy.wait_send()
+    if TIE_RELAY:
+        for way in range(2):
+            tie_copy(way).wait_send()
+            remote(tie_buf.at[way], tie_buf.at[way], tie_out.at[way], far_recv, far).wait_send()
+    n_far = sections - (per_y if TIE_RELAY else 0)
+    remote(text_ref.at[pl.ds(0, n_far)], panel.at[1, pl.ds(0, n_far)], far_send, far_recv, far).wait_send()
+    n_near = sections - 1
+    remote(text_ref.at[pl.ds(0, n_near)], panel.at[0, pl.ds(0, n_near)], near_send, near_recv, far).wait_send()
     for half in range(2):
         for way in range(2):
             for k in range(hops(way, half)):
@@ -210,12 +283,6 @@
 def local(dims, text_emb, covariate, labels, logit_scale, logit_bias):
     n_z, y_lo, per_y = dims
     sections = y_lo * per_y
-    plane = 2 * sections
-    groups = [[at * plane + i for i in range(plane)] for at in range(n_z)]
-    panel = lax.all_to_all(
-        jnp.concatenate([text_emb, text_emb], 0), ("blk", "section"),
-        split_axis=0, concat_axis=0, tiled=True, axis_index_groups=groups,
-    )
     cov_own = covariate[0]
     rows_dev, width = cov_own.shape
     rows_txt = labels.shape[1]
@@ -234,6 +301,8 @@
         in_specs=[vmem, vmem, vmem, smem, smem],
         out_specs=(vmem, vmem),
         scratch_shapes=[
+            pltpu.VMEM((2, sections, text_emb.shape[1], width), BF16),
+            pltpu.VMEM((2, per_y // 2, text_emb.shape[1], width), BF16),
             pltpu.VMEM((n_z, 2, half_rows, width), BF16),
             pltpu.VMEM((1, rows_txt), jnp.int32),
             pltpu.VMEM((n_z * rows_dev, 2 * rows_txt), BF16),
@@ -248,11 +317,12 @@
             dma((2, 2, reach)), dma((2, 2, reach)), dma((2, 2, reach)), dma((2, 2, reach)),
             dma((2, PIECES)), dma((2, PIECES)), dma((2, PIECES)), dma((2, PIECES)),
             dma((2,)), dma((2,)),
+            dma((2,)), dma((2,)), dma((2,)), dma((2,)), dma((2,)),
         ],
         compiler_params=pltpu.CompilerParams(
             collective_id=0, has_side_effects=True, vmem_limit_bytes=48 * 1024 * 1024
         ),
-    )(panel, cov_own, labels, logit_scale, logit_bias)
+    )(text_emb, cov_own, labels, logit_scale, logit_bias)
     return text_grad[None], cov_grad[None]
 
 

time: 115 us -> 86.5 us (0.75)
  waiting for transfers between devices: 27.6 us -> 0 us
  starting transfers between devices: 13.7 us -> 0 us
  Pallas kernels: 67.7 us -> 80.1 us
  local copies, waits for them, and re-layouts: 1.68 us -> 4.29 us
  other arithmetic: 2.26 us -> 0 us
    all_to_all x1 -> x0, waiting for transfers between devices: 27.6 us -> none  [local(): lax.all_to_all(jnp.concatenate([text_emb, text_emb], 0), ('blk', 'section...]
    all_to_all x1 -> x0, starting transfers between devices: 13.7 us -> none  [local(): lax.all_to_all(jnp.concatenate([text_emb, text_emb], 0), ('blk', 'section...]
    pallas_call x1, Pallas kernels: 67.7 us -> 80.1 us  [local(): pl.pallas_call(functools.partial(kernel, dims), out_shape=(jax.ShapeDtype...]
    unnamed x6 -> x8, local copies, waits for them, and re-layouts: 1.68 us -> 4.29 us
    concatenate x1 -> x0, other arithmetic: 2.26 us -> none  [local(): jnp.concatenate([text_emb, text_emb], 0)]
  transfers between devices with their start and end apart: 1 -> 0, of which waited for: 1 -> 0; matrix products, arithmetic and copies ran while one was open for 0% -> 0% of each run, Pallas kernels for 0% -> 0%
where the time goes in v2:
time: 86.5 us; the launch traced here: 86.3 us
  Pallas kernels  80.1 us (93%)
  local copies, waits for them, and re-layouts  4.29 us (5%)
  between operations  1.94 us (2%)
    pallas_call x1, Pallas kernels, local(): pl.pallas_call(functools.partial(kernel, dims), out_shape=(jax.ShapeDtype...  80.1 us
    unnamed x8, local copies, waits for them, and re-layouts  4.29 us

profile of v2, /device:TPU:6, one launch (start us, length us, event | category | flops | bytes accessed | tf_op | source)
XLA Modules:
  0.0 86.3 jit_solution(681421681566551496)
XLA Ops:
  1.9 0.0 copy-start.2
  1.9 0.7 copy-done.2
  2.6 0.0 copy-start
  2.6 1.0 %copy-done = bf16[32,8,1024]{2,1,0:T(8,128)(2,1)S(1)} copy-done((bf16[32,8,1024]{2,1,0:T(8,128)(2,1)S(1)}, bf16[32,8,1024]{2,1,0:T(8,128)(2,1)}, u32[]{:S(2)}) %copy-start) | copy-done | bytes 524312
  3.6 0.0 copy-start.1
  3.6 0.9 %copy-done.1 = bf16[1,64,1024]{2,1,0:T(8,128)(2,1)S(1)} copy-done((bf16[1,64,1024]{2,1,0:T(8,128)(2,1)S(1)}, bf16[1,64,1024]{2,1,0:T(8,128)(2,1)}, u32[]{:S(2)}) %copy-start.1) | copy-done | bytes 131096
  4.5 80.1 %shard_map.68 = (f32[256,1024]{1,0:T(8,128)S(1)}, f32[64,1024]{1,0:T(8,128)S(1)}) custom-call(bf16[32,8,1024]{2,1,0:T(8,128)(2,1)S(1)} %copy-done, bf16[64,1024]{1,0:T(8,128)(2,1)S(1)} %bitcast.5, s32[1,256]{1,0:T(1,128)S(1)} %copy-done.2, f32[1]{0:T(128)S(6)} %copy.9.scale_ref, f32[1]{0:T(128)S(6)} %copy.10.bias_ref), custom_call_target="tpu_custom_call" | custom-call | tf_op jit(solution)/shard_map/pallas_call | solution.py:295
  84.6 1.0 %copy.11 = f32[1,256,1024]{2,1,0:T(8,128)} copy(f32[1,256,1024]{2,1,0:T(8,128)S(1)} %bitcast.3) | data formatting | bytes 2097152
  85.6 0.7 copy.12
Async XLA Ops:
  1.9 0.7 copy-start.2
  2.6 1.0 %copy-start = (bf16[32,8,1024]{2,1,0:T(8,128)(2,1)S(1)}, bf16[32,8,1024]{2,1,0:T(8,128)(2,1)}, u32[]{:S(2)}) copy-start(bf16[32,8,1024]{2,1,0:T(8,128)(2,1)} %text_ref.1) | copy-start | bytes 1572868
  3.6 0.9 %copy-start.1 = (bf16[1,64,1024]{2,1,0:T(8,128)(2,1)S(1)}, bf16[1,64,1024]{2,1,0:T(8,128)(2,1)}, u32[]{:S(2)}) copy-start(bf16[1,64,1024]{2,1,0:T(8,128)(2,1)} %param.6) | copy-start | bytes 393220
